TPU v7x, 32 devices: a whole 2x2x4 slice. The times are simulated.
32 devices in a mesh: row: 4 (over z), col: 8 (over y, x, core).
Axes of the slice: x: 2, y: 2, z: 4, core: 2. Of those that a mesh axis runs over, the one named last changes fastest.
Arguments:
- grad_first: float32 [4096, 20480], P('row', 'col'), may hold values from -1000 to 1000
- grad_second: float32 [4096, 20480], P('row', 'col'), may hold values from -1000 to 1000
Outputs:
- update: float32 [4096, 20480], P('row', 'col')
All inputs are finite; a program needn't handle non-finite values.
Results may differ from a plain program's by a relative error of at most 0.00014.
Values sent between devices are 32-bit elements; how exact they have to be, the bound alone decides.
A program may use at most 128 MiB of HBM per device.

v0:
```python
import jax
import jax.numpy as jnp
from jax import lax
from jax.sharding import PartitionSpec as P

D = 4096
FF = 20480
BLOCK = 256
ITERS = 6


damping = 0.001


def batched(left_mat, right_mat):
    return jnp.einsum("kij,kjl->kil", left_mat, right_mat, precision=lax.Precision.HIGHEST)


def newton_roots(statistic):
    width = statistic.shape[-1]
    identity = jnp.eye(width, dtype=jnp.float32)
    damped = statistic + damping * identity
    frob_norm = jnp.sqrt(jnp.sum(damped * damped, axis=(1, 2)))
    scaled = damped / frob_norm[:, None, None]
    current = identity[None] * lax.rsqrt(jnp.sqrt(frob_norm))[:, None, None]
    for iteration in range(ITERS):
        factor = (5.0 * identity - scaled) / 4.0
        current = batched(current, factor)
        square = batched(factor, factor)
        scaled = batched(batched(square, square), scaled)
    return current


def owned_roots(statistic, owner, groups):
    total = statistic.shape[0]
    slots = (total + groups - 1) // groups
    picks = owner + groups * jnp.arange(slots, dtype=jnp.int32)
    valid = picks < total
    chosen = jnp.take(statistic, jnp.minimum(picks, total - 1), axis=0)
    selector = (
        (jnp.arange(total, dtype=jnp.int32)[:, None] == picks[None, :]) & valid[None, :]
    ).astype(jnp.float32)
    return jnp.einsum(
        "bk,kij->bij", selector, newton_roots(chosen), precision=lax.Precision.HIGHEST
    )


def body(grad_first, grad_second):
    row_count = grad_first.shape[0]
    col_count = grad_first.shape[1]
    left_total = row_count // BLOCK
    right_total = col_count // BLOCK
    col_devices = lax.axis_size("col")
    row_devices = lax.axis_size("row")
    col_index = lax.axis_index("col")
    right_slots = (right_total + row_devices - 1) // row_devices
    left_state = jnp.zeros((left_total, BLOCK, BLOCK), jnp.float32)
    right_state = jnp.zeros((right_slots, BLOCK, BLOCK), jnp.float32)
    update = jnp.zeros((row_count, col_count), jnp.float32)
    for gradient in (grad_first, grad_second):
        row_blocks = gradient.reshape(left_total, BLOCK, col_count)
        col_blocks = gradient.reshape(row_count, right_total, BLOCK)
        left_part = jnp.einsum(
            "bik,bjk->bij", row_blocks, row_blocks, precision=lax.Precision.HIGHEST
        )
        right_part = jnp.einsum(
            "kbi,kbj->bij", col_blocks, col_blocks, precision=lax.Precision.HIGHEST
        )
        left_state = left_state + lax.psum(left_part, "col") / FF
        left_factor = lax.psum(owned_roots(left_state, col_index, col_devices), "col")
        padding = jnp.zeros((right_slots * row_devices - right_total, BLOCK, BLOCK), jnp.float32)
        padded = jnp.concatenate([right_part, padding], axis=0)
        ordered = (
            padded.reshape(right_slots, row_devices, BLOCK, BLOCK)
            .transpose(1, 0, 2, 3)
            .reshape(row_devices * right_slots, BLOCK, BLOCK)
        )
        right_state = (
            right_state + lax.psum_scatter(ordered, "row", scatter_dimension=0, tiled=True) / D
        )
        gathered = lax.all_gather(newton_roots(right_state), "row", axis=0, tiled=True)
        right_factor = (
            gathered.reshape(row_devices, right_slots, BLOCK, BLOCK)
            .transpose(1, 0, 2, 3)
            .reshape(right_slots * row_devices, BLOCK, BLOCK)[:right_total]
        )
        halfway = jnp.einsum(
            "bij,bjk->bik", left_factor, row_blocks, precision=lax.Precision.HIGHEST
        ).reshape(row_count, right_total, BLOCK)
        update = update + jnp.einsum(
            "kbi,bij->kbj", halfway, right_factor, precision=lax.Precision.HIGHEST
        ).reshape(row_count, col_count)
    return update


def solution(mesh):
    in_specs = (P("row", "col"), P("row", "col"))
    out_specs = P("row", "col")
    return jax.shard_map(body, mesh=mesh, in_specs=in_specs, out_specs=out_specs, check_vma=False)
```

profile of v0, /device:TPU:0, one launch (start us, length us, event | category | flops | bytes accessed | tf_op | source)
XLA Modules:
  0.0 434.1 jit_solution(6471430727540527559)
XLA Ops:
  7.4 15.2 %fusion.300 = f32[4,256,256]{2,1,0:T(8,128)} fusion(f32[4,256,2560]{2,1,0:T(8,128)} %bitcast.161), kind=kOutput, calls=%fused_computation.318 | convolution fusion | flops 8053063680 | bytes 11534336 | tf_op jit(solution)/shard_map/bik,bjk->bij/dot_general | solution.py:63
  22.6 10.7 %fusion.322 = f32[4,256,256]{2,1,0:T(8,128)} fusion(f32[4,256,2560]{2,1,0:T(8,128)S(1)} %bitcast.160), kind=kOutput, calls=%fused_computation.340 | convolution fusion | flops 8053063680 | bytes 11534336 | tf_op jit(solution)/shard_map/bik,bjk->bij/dot_general | solution.py:63
  33.4 11.7 %copy.27 = f32[1024,2560]{0,1:T(8,128)} copy(f32[1024,2560]{1,0:T(8,128)} %param.4) | data formatting | bytes 20971520 | tf_op args[0]
  45.1 16.9 %fusion.290 = f32[10,256,256]{2,1,0:T(8,128)S(1)} fusion(f32[1024,10,256]{0,2,1:T(8,128)} %bitcast.163), kind=kOutput, calls=%fused_computation.308 | convolution fusion | flops 8053063680 | bytes 13107200 | tf_op jit(solution)/shard_map/kbi,kbj->bij/dot_general | solution.py:66
  62.3 2.0 copy.29
  64.4 11.6 %copy.33 = f32[1024,2560]{0,1:T(8,128)} copy(f32[1024,2560]{1,0:T(8,128)} %param.5) | data formatting | bytes 20971520 | tf_op args[1]
  76.0 16.9 %fusion.311 = f32[10,256,256]{2,1,0:T(8,128)S(1)} fusion(f32[1024,10,256]{0,2,1:T(8,128)} %bitcast.164), kind=kOutput, calls=%fused_computation.329 | convolution fusion | flops 8053063680 | bytes 13107200 | tf_op jit(solution)/shard_map/kbi,kbj->bij/dot_general | solution.py:66
  93.2 2.1 copy.35
  95.9 2.2 all-reduce.9.cloned.1.call-done
  98.1 1.3 broadcast_multiply_fusion.2
  99.4 1.7 multiply_reduce_fusion.3
  101.9 1.0 broadcast_divide_fusion.1
  108.2 1.1 fusion.95
  116.5 1.4 fusion.116
  122.5 1.6 broadcast_multiply_fusion.1
  124.2 3.4 reduce-scatter.3.cloned.1.call-done
  127.6 62.4 %reduce-scatter.5.cloned.1.call-done = f32[3,256,256]{2,1,0:T(8,128)} async-done(((f32[12,256,256]{2,1,0:T(8,128)}), f32[3,256,256]{2,1,0:T(8,128)}) %reduce-scatter.5.cloned.1.call-update) | async-done | bytes 786448 | tf_op jit(solution)/shard_map/reduce_scatter | solution.py:79
  190.0 1.7 multiply_reduce_fusion.1
  191.8 2.6 fusion.15
  194.3 0.9 fusion.291
  195.2 2.1 fusion.288
  197.4 1.0 fusion.16
  199.3 0.9 fusion.293
  200.2 1.0 fusion.18
  201.2 0.9 fusion.294
  202.1 0.9 fusion.295
  203.0 1.0 fusion.20
  204.1 0.9 fusion.296
  205.0 0.9 fusion.297
  205.9 1.4 fusion.22
  208.2 0.9 fusion.8
  209.1 1.1 fusion.13
  210.2 0.9 fusion.17
  211.1 0.9 fusion.19
  212.3 1.0 fusion.24
  214.2 0.9 fusion.313
  215.1 1.0 fusion.25
  216.1 0.9 fusion.21
  217.0 0.9 fusion.23
  218.0 2.0 fusion.299
  221.0 0.9 fusion.315
  221.9 1.0 fusion.27
  222.9 0.9 fusion.316
  223.8 0.9 fusion.317
  224.7 1.0 fusion.29
  226.6 0.9 fusion.319
  227.5 1.0 fusion.31
  228.5 1.0 fusion.11
  230.4 0.9 fusion.7
  231.3 1.4 fusion.26
  232.7 0.9 fusion.28
  233.6 0.9 fusion.30
  234.6 0.9 fusion.32
  235.5 1.8 fusion.321
  237.4 14.8 %fusion.332 = f32[4,256,2560]{2,1,0:T(8,128)} fusion(f32[4,256,256]{2,1,0:T(8,128)} %get-tuple-element.21, f32[4,256,2560]{2,1,0:T(8,128)} %bitcast.157), kind=kOutput, calls=%fused_computation.350 | convolution fusion | flops 8053063680 | bytes 22020096 | tf_op jit(solution)/shard_map/bij,bjk->bik/dot_general | solution.py:87
  252.2 14.4 %reshape.442 = f32[1024,10,256]{2,1,0:T(8,128)} reshape(f32[4,256,2560]{2,1,0:T(8,128)} %fusion.332) | data formatting | bytes 20971520 | tf_op jit(solution)/shard_map/reshape | solution.py:89
  266.6 14.4 %fusion.310 = f32[4,256,2560]{2,1,0:T(8,128)} fusion(f32[4,256,256]{2,1,0:T(8,128)S(1)} %copy-done.2, f32[4,256,2560]{2,1,0:T(8,128)} %bitcast.162), kind=kOutput, calls=%fused_computation.328 | convolution fusion | flops 8053063680 | bytes 22020096 | tf_op jit(solution)/shard_map/bij,bjk->bik/dot_general | solution.py:87
  281.0 14.3 %reshape.441 = f32[1024,10,256]{2,1,0:T(8,128)} reshape(f32[4,256,2560]{2,1,0:T(8,128)} %fusion.310) | data formatting | bytes 20971520 | tf_op jit(solution)/shard_map/reshape | solution.py:89
  295.3 2.4 copy.30
  297.7 49.1 %all-gather.5.cloned.1.call-done = f32[12,256,256]{2,1,0:T(8,128)} async-done(((f32[3,256,256]{2,1,0:T(8,128)}), f32[12,256,256]{2,1,0:T(8,128)}) %all-gather.5.cloned.1.call-update) | async-done | bytes 3145744 | tf_op jit(solution)/shard_map/all_gather | solution.py:81
  346.8 3.5 copy.36
  350.4 23.2 %fusion = f32[10,256,1024]{2,1,0:T(8,128)} fusion(f32[12,256,256]{1,2,0:T(8,128)} %bitcast.173, f32[1024,10,256]{2,1,0:T(8,128)} %reshape.442), kind=kOutput, calls=%fused_computation | convolution fusion | flops 8053063680 | bytes 24117248 | tf_op jit(solution)/shard_map/kbi,bij->kbj/dot_general | solution.py:90
  373.6 41.2 %fusion.4 = f32[10,256,1024]{2,1,0:T(8,128)} fusion(f32[10,256,1024]{2,1,0:T(8,128)} %fusion, f32[12,256,256]{1,2,0:T(8,128)S(1)} %bitcast.172, f32[1024,10,256]{2,1,0:T(8,128)} %reshape.441), kind=kOutput, calls=%fused_computation.4 | convolution fusion | flops 8055685120 | bytes 34603008 | tf_op jit(solution)/shard_map/kbi,bij->kbj/dot_general | solution.py:90
  414.8 11.4 %copy.39 = f32[1024,2560]{1,0:T(8,128)} copy(f32[1024,2560]{0,1:T(8,128)} %bitcast.169) | data formatting | bytes 20971520 | tf_op jit(solution)/shard_map/add | solution.py:90
  (81 shorter events, 22.9 us)
Async XLA Ops:
  7.4 90.7 %all-reduce.9.cloned.1.call-start = ((), (), s32[]{:S(2)}) async-start(), calls=%async_computation.7 | async-start | bytes 4194304 | tf_op jit(solution)/shard_map/psum | solution.py:69
  7.4 15.2 %slice-start = ((s8[10485760]{0:T(1024)(128)(4,1)}), s8[4194304]{0:T(1024)(128)(4,1)S(1)}, s32[]{:S(2)}) async-start(s8[10485760]{0:T(1024)(128)(4,1)} %bitcast.158), calls=%async_computation.8 | async-start | bytes 8388608
  7.4 15.2 %slice-start.1 = ((s8[10485760]{0:T(1024)(128)(4,1)}), s8[4194304]{0:T(1024)(128)(4,1)S(1)}, s32[]{:S(2)}) async-start(s8[10485760]{0:T(1024)(128)(4,1)} %bitcast.158), calls=%async_computation.9 | async-start | bytes 8388608
  7.4 15.2 %slice-start.2 = ((s8[10485760]{0:T(1024)(128)(4,1)}), s8[2097152]{0:T(1024)(128)(4,1)S(1)}, s32[]{:S(2)}) async-start(s8[10485760]{0:T(1024)(128)(4,1)} %bitcast.158), calls=%async_computation.10 | async-start | bytes 4194304
  33.4 94.2 %reduce-scatter.3.cloned.1.call-start = ((), (), s32[]{:S(2)}) async-start(), calls=%async_computation.2 | async-start | bytes 3932160 | tf_op jit(solution)/shard_map/reduce_scatter | solution.py:79
  64.3 125.7 %reduce-scatter.5.cloned.1.call-start = ((), (), s32[]{:S(2)}) async-start(), calls=%async_computation.4 | async-start | bytes 3932160 | tf_op jit(solution)/shard_map/reduce_scatter | solution.py:79
  95.2 142.1 %all-reduce.7.cloned.1.call-start = ((), (), s32[]{:S(2)}) async-start(), calls=%async_computation.6 | async-start | bytes 4194304 | tf_op jit(solution)/shard_map/psum | solution.py:70
  124.1 171.2 %all-gather.3.cloned.1.call-start = ((), (), s32[]{:S(2)}) async-start(), calls=%async_computation.3 | async-start | bytes 3932160 | tf_op jit(solution)/shard_map/all_gather | solution.py:81
  200.2 8.9 %copy-start = (f32[3,256,256]{2,1,0:T(8,128)S(1)}, f32[3,256,256]{2,1,0:T(8,128)}, u32[]{:S(2)}) copy-start(f32[3,256,256]{2,1,0:T(8,128)} %reduce-scatter.3.cloned.1.call-done) | copy-start | bytes 2359300
  204.1 8.0 %copy-start.1 = (f32[3,256,256]{2,1,0:T(8,128)S(1)}, f32[3,256,256]{2,1,0:T(8,128)}, u32[]{:S(2)}) copy-start(f32[3,256,256]{2,1,0:T(8,128)} %reduce-scatter.5.cloned.1.call-done) | copy-start | bytes 2359300
  220.0 126.8 %all-gather.5.cloned.1.call-start = ((), (), s32[]{:S(2)}) async-start(), calls=%async_computation.5 | async-start | bytes 3932160 | tf_op jit(solution)/shard_map/all_gather | solution.py:81
  252.2 14.4 %copy-start.2 = (f32[4,256,256]{2,1,0:T(8,128)S(1)}, f32[4,256,256]{2,1,0:T(8,128)}, u32[]{:S(2)}) copy-start(f32[4,256,256]{2,1,0:T(8,128)} %get-tuple-element.22) | copy-start | bytes 3145732
Sparse Core Ops, SparseCore 0:
  33.5 64.5 all-reduce.8
  124.2 62.1 all-reduce.6
Sparse Core Ops, SparseCore 1:
  64.4 63.1 reduce-scatter.2
  129.8 60.2 reduce-scatter.4
  220.1 63.1 all-gather.2
  284.9 61.9 all-gather.4
where the time goes:
time: 440 us; the launch traced here: 434 us
  matrix products  217 us (49%)
  waiting for transfers between devices  117 us (27%)
  local copies, waits for them, and re-layouts  73.9 us (17%)
  between operations  17.6 us (4%)
  other arithmetic  7.64 us (2%)
    reduce_scatter x2, waiting for transfers between devices, body(): lax.psum_scatter(ordered, 'row', scatter_dimension=0, tiled=True) / D  65.8 us
    dot_general x2, matrix products, body(): jnp.einsum('kbi,bij->kbj', halfway, right_factor, precision=lax.Precision...  64.5 us
    dot_general x84, matrix products, batched(): jnp.einsum('kij,kjl->kil', left_mat, right_mat, precision=lax.Precision.H...  63.4 us
    all_gather x2, waiting for transfers between devices, body(): lax.all_gather(newton_roots(right_state), 'row', axis=0, tiled=True)  49.1 us
    dot_general x2, matrix products, body(): jnp.einsum('kbi,kbj->bij', col_blocks, col_blocks, precision=lax.Precisio...  33.9 us
    dot_general x2, matrix products, body(): jnp.einsum('bij,bjk->bik', left_factor, row_blocks, precision=lax.Precisi...  29.2 us
    reshape x2, local copies, waits for them, and re-layouts, body(): halfway = jnp.einsum('bij,bjk->bik', left_factor, row_blocks, precision=l...  28.7 us
    dot_general x2, matrix products, body(): jnp.einsum('bik,bjk->bij', row_blocks, row_blocks, precision=lax.Precisio...  25.9 us
  transfers between devices with their start and end apart: 6, of which 4 were waited for; matrix products, arithmetic and copies ran while one was open for 44% of the time, Pallas kernels for 0%

commit v1 on v0

v1 whole, which is shorter than its diff:
```python
import functools

import jax
import jax.numpy as jnp
from jax import lax
from jax.experimental import pallas as pl
from jax.experimental.pallas import tpu as pltpu
from jax.sharding import PartitionSpec as P

BLOCK = 256
HALF = 128
PACKED = BLOCK + 8
ITERS = 6
damping = 0.001
VMEM_LIMIT = 56 * 1024 * 1024


def split(value):
    high = value.astype(jnp.bfloat16)
    low = (value - high.astype(jnp.float32)).astype(jnp.bfloat16)
    return high, low


def dot(left, right, dims=(((1,), (0,)), ((), ()))):
    return lax.dot_general(left, right, dims, preferred_element_type=jnp.float32)


def product(left, right):
    return dot(
        jnp.concatenate([left[0], left[0], left[1]], axis=1),
        jnp.concatenate([right[0], right[1], right[0]], axis=0),
    )


def indices():
    rows = lax.broadcasted_iota(jnp.int32, (HALF, HALF), 0)
    cols = lax.broadcasted_iota(jnp.int32, (HALF, HALF), 1)
    return rows, cols


def pack(write, block):
    rows, cols = indices()
    first, last = block[:HALF, :HALF], block[HALF:, HALF:]
    write(0, HALF, block[:HALF, HALF:])
    write(HALF, HALF, jnp.where(rows <= cols, first, last))
    diagonal = jnp.sum(jnp.where(rows == cols, last, 0.0), axis=0, keepdims=True)
    write(BLOCK, 8, jnp.broadcast_to(diagonal, (8, HALF)))


def unpack(packed):
    rows, cols = indices()
    off = packed[:HALF]
    tile = packed[HALF:BLOCK]
    turned = tile.T
    first = jnp.where(rows <= cols, tile, turned)
    last = jnp.where(rows > cols, tile, jnp.where(rows < cols, turned, packed[BLOCK : BLOCK + 1]))
    return jnp.concatenate(
        [jnp.concatenate([first, off], axis=1), jnp.concatenate([off.T, last], axis=1)], axis=0
    )


def writer(ref, *lead):
    def write(start, size, value):
        ref[(*lead, pl.ds(start, size), slice(None))] = value

    return write


def left_stat_kernel(g1_ref, g2_ref, out_ref):
    total = None
    for step, ref in enumerate((g1_ref, g2_ref)):
        high, low = split(ref[...])
        both = dot(high, jnp.concatenate([high, low], axis=0), (((1,), (1,)), ((), ())))
        cross = both[:, BLOCK:]
        part = both[:, :BLOCK] + (cross + cross.T)
        total = part if total is None else total + part
        pack(writer(out_ref, step, 0), total)


def right_stat_kernel(g1_ref, g2_ref, out_ref):
    total = None
    for step, ref in enumerate((g1_ref, g2_ref)):
        high, low = split(ref[...])
        both = dot(high.T, jnp.concatenate([high, low], axis=1))
        cross = both[:, BLOCK:]
        part = both[:, :BLOCK] + (cross + cross.T)
        total = part if total is None else total + part
        pack(writer(out_ref, step, 0), total)


def stats(kernel, grads, count, tile, index):
    flops = 8 * grads[0].size * BLOCK
    return pl.pallas_call(
        kernel,
        grid=(count,),
        in_specs=[pl.BlockSpec(tile, index)] * 2,
        out_specs=pl.BlockSpec((2, 1, PACKED, HALF), lambda i: (0, i, 0, 0)),
        out_shape=jax.ShapeDtypeStruct((2, count, PACKED, HALF), jnp.float32),
        compiler_params=pltpu.CompilerParams(vmem_limit_bytes=VMEM_LIMIT),
        cost_estimate=pl.CostEstimate(
            flops=flops, bytes_accessed=8 * grads[0].size, transcendentals=0
        ),
    )(*grads)


def root_kernel(count, scale, stat_ref, out_ref, x_ref, m_ref):
    rows = lax.broadcasted_iota(jnp.int32, (BLOCK, BLOCK), 0)
    cols = lax.broadcasted_iota(jnp.int32, (BLOCK, BLOCK), 1)
    identity = jnp.where(rows == cols, 1.0, 0.0)

    def factor_of(scaled):
        return (5.0 * identity - scaled) / 4.0

    def advance(factor_parts, scaled):
        square = product(factor_parts, factor_parts)
        square_parts = split(square)
        fourth = product(square_parts, square_parts)
        return product(split(fourth), split(scaled))

    for slot in range(count):
        damped = unpack(stat_ref[slot]) * scale + damping * identity
        total = jnp.sum(jnp.sum(damped * damped, axis=0, keepdims=True), axis=1, keepdims=True)
        norm = jnp.sqrt(total)
        scaled = damped / norm
        factor = factor_of(scaled)
        x_ref[slot] = factor * lax.rsqrt(jnp.sqrt(norm))
        m_ref[slot] = advance(split(factor), scaled)

    def step(iteration, carry):
        for slot in range(count):
            scaled = m_ref[slot]
            parts = split(factor_of(scaled))
            x_ref[slot] = product(split(x_ref[slot]), parts)
            m_ref[slot] = advance(parts, scaled)
        return carry

    lax.fori_loop(0, ITERS - 2, step, 0)
    for slot in range(count):
        result = product(split(x_ref[slot]), split(factor_of(m_ref[slot])))
        pack(writer(out_ref, slot), result)


def roots(statistic, scale):
    count = statistic.shape[0]
    return pl.pallas_call(
        functools.partial(root_kernel, count, scale),
        out_shape=jax.ShapeDtypeStruct(statistic.shape, jnp.float32),
        scratch_shapes=[pltpu.VMEM((count, BLOCK, BLOCK), jnp.float32)] * 2,
        compiler_params=pltpu.CompilerParams(vmem_limit_bytes=VMEM_LIMIT),
        cost_estimate=pl.CostEstimate(
            flops=count * 20 * 6 * BLOCK**3, bytes_accessed=2 * statistic.size * 4, transcendentals=0
        ),
    )(statistic)


def left_apply_kernel(g1_ref, g2_ref, l1_ref, l2_ref, high_ref, low_ref):
    for step, (g_ref, l_ref) in enumerate(((g1_ref, l1_ref), (g2_ref, l2_ref))):
        half = product(split(unpack(l_ref[0])), split(g_ref[...]))
        high, low = split(half)
        high_ref[step] = high
        low_ref[step] = low


def left_apply(grads, packed, count):
    rows, cols = grads[0].shape
    tiles = 2 if cols % (2 * HALF) == 0 else 1
    width = cols // tiles
    root_spec = lambda first: pl.BlockSpec((1, PACKED, HALF), lambda b, t: (first + b, 0, 0))
    out_spec = pl.BlockSpec((2, BLOCK, width), lambda b, t: (0, b, t))
    return pl.pallas_call(
        left_apply_kernel,
        grid=(count, tiles),
        in_specs=[pl.BlockSpec((BLOCK, width), lambda b, t: (b, t))] * 2
        + [root_spec(0), root_spec(count)],
        out_specs=[out_spec] * 2,
        out_shape=[jax.ShapeDtypeStruct((2, rows, cols), jnp.bfloat16)] * 2,
        compiler_params=pltpu.CompilerParams(vmem_limit_bytes=VMEM_LIMIT),
        cost_estimate=pl.CostEstimate(
            flops=12 * rows * cols * BLOCK, bytes_accessed=16 * rows * cols, transcendentals=0
        ),
    )(*grads, packed, packed)


def right_apply_kernel(high_ref, low_ref, r1_ref, r2_ref, out_ref):
    lefts, rights = [], []
    for step, r_ref in enumerate((r1_ref, r2_ref)):
        high, low = split(unpack(r_ref[0]))
        lefts += [high_ref[step], high_ref[step], low_ref[step]]
        rights += [high, low, high]
    out_ref[...] = dot(jnp.concatenate(lefts, axis=1), jnp.concatenate(rights, axis=0))


def right_apply(high, low, packed, count):
    _, rows, cols = high.shape
    root_spec = lambda first: pl.BlockSpec((1, PACKED, HALF), lambda j: (first + j, 0, 0))
    half_spec = pl.BlockSpec((2, rows, BLOCK), lambda j: (0, 0, j))
    return pl.pallas_call(
        right_apply_kernel,
        grid=(count,),
        in_specs=[half_spec, half_spec, root_spec(0), root_spec(count)],
        out_specs=pl.BlockSpec((rows, BLOCK), lambda j: (0, j)),
        out_shape=jax.ShapeDtypeStruct((rows, cols), jnp.float32),
        compiler_params=pltpu.CompilerParams(vmem_limit_bytes=VMEM_LIMIT),
        cost_estimate=pl.CostEstimate(
            flops=12 * rows * cols * BLOCK, bytes_accessed=12 * rows * cols, transcendentals=0
        ),
    )(high, low, packed, packed)


def scatter(packed, axis):
    devices = lax.axis_size(axis)
    flat = packed.reshape(-1, PACKED, HALF)
    extra = -flat.shape[0] % devices
    if extra:
        flat = jnp.concatenate([flat, jnp.zeros((extra, PACKED, HALF), jnp.float32)], axis=0)
    return lax.psum_scatter(flat, axis, scatter_dimension=0, tiled=True)


def body(grad_first, grad_second):
    grads = (grad_first, grad_second)
    rows, cols = grad_first.shape
    left_count, right_count = rows // BLOCK, cols // BLOCK
    left_scale = 1.0 / (cols * lax.axis_size("col"))
    right_scale = 1.0 / (rows * lax.axis_size("row"))
    left_part = stats(left_stat_kernel, grads, left_count, (BLOCK, cols), lambda i: (i, 0))
    right_part = stats(right_stat_kernel, grads, right_count, (rows, BLOCK), lambda i: (0, i))
    left_sum = scatter(left_part, "col")
    right_sum = scatter(right_part, "row")
    left_roots = lax.all_gather(roots(left_sum, left_scale), "col", axis=0, tiled=True)
    right_own = roots(right_sum, right_scale)
    right_roots = lax.all_gather(right_own, "row", axis=0, tiled=True)
    high, low = left_apply(grads, left_roots, left_count)
    return right_apply(high, low, right_roots, right_count)


def solution(mesh):
    in_specs = (P("row", "col"), P("row", "col"))
    out_specs = P("row", "col")
    return jax.shard_map(body, mesh=mesh, in_specs=in_specs, out_specs=out_specs, check_vma=False)
```

time: 440 us -> 220 us (0.50); the launches traced: 434 us -> 219 us
  matrix products: 217 us -> 0 us
  Pallas kernels: 0 us -> 93.5 us
  local copies, waits for them, and re-layouts: 73.9 us -> 0 us
  other arithmetic: 7.64 us -> 0 us
  waiting for transfers between devices: 117 us -> 112 us
  between operations: 17.6 us -> 13.1 us
    dot_general x92 -> x0, matrix products: 217 us -> none  [the longest x2 64.5 us: body(): jnp.einsum('kbi,bij->kbj', halfway, right_factor, precision=lax.Precision...]
    pallas_call x0 -> x6, Pallas kernels: none -> 93.5 us  [the longest x2 29.2 us: roots(): pl.pallas_call(functools.partial(root_kernel, count, scale), out_shape=ja...]
    unnamed x6, waiting for transfers between devices: 0.1 us -> 72.6 us
    reduce_scatter x2 -> x0, waiting for transfers between devices: 65.8 us -> none  [body(): lax.psum_scatter(ordered, 'row', scatter_dimension=0, tiled=True) / D]
    reshape x5 -> x0, local copies, waits for them, and re-layouts: 36.7 us -> none  [the longest x2 28.7 us: body(): halfway = jnp.einsum('bij,bjk->bik', left_factor, row_blocks, precision=l...]
    unnamed x14 -> x0, local copies, waits for them, and re-layouts: 23.3 us -> none
    add x1 -> x0, local copies, waits for them, and re-layouts: 11.4 us -> none  [body(): update + jnp.einsum('kbi,bij->kbj', halfway, right_factor, precision=lax....]
    all_gather x2, waiting for transfers between devices: 49.1 us -> 39.4 us  [the longest x1 36.8 us: body(): right_roots = lax.all_gather(right_own, 'row', axis=0, tiled=True)]
  transfers between devices with their start and end apart: 6 -> 4, of which waited for: 4 -> 4; matrix products, arithmetic and copies ran while one was open for 44% -> 0% of each run, Pallas kernels for 0% -> 30%
where the time goes in v1:
time: 220 us; the launch traced here: 219 us
  waiting for transfers between devices  112 us (51%)
  Pallas kernels  93.5 us (42%)
  between operations  13.1 us (6%)
    unnamed x6, waiting for transfers between devices  72.6 us
    all_gather x1, waiting for transfers between devices, body(): right_roots = lax.all_gather(right_own, 'row', axis=0, tiled=True)  36.8 us
    pallas_call x2, Pallas kernels, roots(): pl.pallas_call(functools.partial(root_kernel, count, scale), out_shape=ja...  29.2 us
    pallas_call x2, Pallas kernels, stats(): pl.pallas_call(kernel, grid=(count,), in_specs=[pl.BlockSpec(tile, index)...  25.7 us
    pallas_call x1, Pallas kernels, left_apply(): pl.pallas_call(left_apply_kernel, grid=(count, tiles), in_specs=[pl.Block...  20.8 us
    pallas_call x1, Pallas kernels, right_apply(): pl.pallas_call(right_apply_kernel, grid=(count,), in_specs=[half_spec, ha...  17.8 us
  transfers between devices with their start and end apart: 4, of which 4 were waited for; matrix products, arithmetic and copies ran while one was open for 0% of the time, Pallas kernels for 30%

profile of v1, /device:TPU:0, one launch (start us, length us, event | category | flops | bytes accessed | tf_op | source)
XLA Modules:
  0.0 218.9 jit_solution(3310970234850680311)
XLA Ops:
  6.5 0.0 reduce-scatter.7.cloned.1.call-start
  6.5 11.1 %shard_map.28 = f32[2,4,264,128]{3,2,1,0:T(8,128)} custom-call(f32[1024,2560]{1,0:T(8,128)} %g1_ref.5, f32[1024,2560]{1,0:T(8,128)} %g2_ref.5), custom_call_target="tpu_custom_call" | custom-call | flops 5368709120 | bytes 20971520 | tf_op jit(solution)/shard_map/pallas_call | solution.py:93
  17.6 0.0 reduce-scatter.7.cloned.1.call-update
  17.6 0.0 reduce-scatter.9.cloned.1.call-start
  17.7 14.7 %shard_map.31 = f32[2,10,264,128]{3,2,1,0:T(8,128)} custom-call(f32[1024,2560]{1,0:T(8,128)} %g1_ref.5, f32[1024,2560]{1,0:T(8,128)} %g2_ref.5), custom_call_target="tpu_custom_call" | custom-call | flops 5368709120 | bytes 20971520 | tf_op jit(solution)/shard_map/pallas_call | solution.py:93
  32.4 0.0 reduce-scatter.9.cloned.1.call-update
  32.4 0.0 all-gather.3.cloned.1.call-start
  32.4 23.5 %reduce-scatter.7.cloned.1.call-done.stat_ref = f32[1,264,128]{2,1,0:T(8,128)} async-done(((f32[8,264,128]{2,1,0:T(8,128)}), f32[1,264,128]{2,1,0:T(8,128)}) %reduce-scatter.7.cloned.1.call-update) | async-done | bytes 135184
  55.9 6.8 %shard_map.29 = f32[1,264,128]{2,1,0:T(8,128)} custom-call(f32[1,264,128]{2,1,0:T(8,128)} %reduce-scatter.7.cloned.1.call-done.stat_ref), custom_call_target="tpu_custom_call" | custom-call | flops 2013265920 | bytes 270336 | tf_op jit(solution)/shard_map/pallas_call | solution.py:145
  62.7 0.0 all-gather.3.cloned.1.call-update
  62.7 0.2 all-gather.5.cloned.1.call-start
  63.0 49.0 %reduce-scatter.9.cloned.1.call-done.stat_ref = f32[5,264,128]{2,1,0:T(8,128)} async-done(((f32[20,264,128]{2,1,0:T(8,128)}), f32[5,264,128]{2,1,0:T(8,128)}) %reduce-scatter.9.cloned.1.call-update) | async-done | bytes 675856
  112.0 22.4 %shard_map.32 = f32[5,264,128]{2,1,0:T(8,128)} custom-call(f32[5,264,128]{2,1,0:T(8,128)} %reduce-scatter.9.cloned.1.call-done.stat_ref), custom_call_target="tpu_custom_call" | custom-call | flops 10066329600 | bytes 1351680 | tf_op jit(solution)/shard_map/pallas_call | solution.py:145
  134.4 0.0 all-gather.5.cloned.1.call-update
  134.4 2.6 %all-gather.3.cloned.1.call-done.l1_ref.l2_ref = f32[8,264,128]{2,1,0:T(8,128)} async-done(((f32[1,264,128]{2,1,0:T(8,128)}), f32[8,264,128]{2,1,0:T(8,128)}) %all-gather.3.cloned.1.call-update) | async-done | bytes 1081360 | tf_op jit(solution)/shard_map/all_gather | solution.py:229
  137.0 20.8 %shard_map.30 = (bf16[2,1024,2560]{2,1,0:T(8,128)(2,1)}, bf16[2,1024,2560]{2,1,0:T(8,128)(2,1)}) custom-call(f32[1024,2560]{1,0:T(8,128)} %g1_ref.5, f32[1024,2560]{1,0:T(8,128)} %g2_ref.5, f32[8,264,128]{2,1,0:T(8,128)} %all-gather.3.cloned.1.call-done.l1_ref.l2_ref, f32[8,264,128]{2,1,0:T(8,128)} %all-gather.3.cloned.1.call-done.l1_ref.l2_ref), custom_call_target="tpu_custom_call" | custom-call | flops 8053063680 | bytes 41943040 | tf_op jit(solution)/shard_map/pallas_call | solution.py:170
  157.8 36.8 %all-gather.5.cloned.1.call-done.r1_ref.r2_ref = f32[20,264,128]{2,1,0:T(8,128)} async-done(((f32[5,264,128]{2,1,0:T(8,128)}), f32[20,264,128]{2,1,0:T(8,128)}) %all-gather.5.cloned.1.call-update) | async-done | bytes 2703376 | tf_op jit(solution)/shard_map/all_gather | solution.py:231
  194.6 17.8 %shard_map.33 = f32[1024,2560]{1,0:T(8,128)} custom-call(bf16[2,1024,2560]{2,1,0:T(8,128)(2,1)} %get-tuple-element.7.high_ref, bf16[2,1024,2560]{2,1,0:T(8,128)(2,1)} %get-tuple-element.8.low_ref, f32[20,264,128]{2,1,0:T(8,128)} %all-gather.5.cloned.1.call-done.r1_ref.r2_ref, f32[20,264,128]{2,1,0:T(8,128)} %all-gather.5.cloned.1.call-done.r1_ref.r2_ref), custom_call_target="tpu_custom_call" | custom-call | flops 8053063680 | bytes 31457280 | tf_op jit(solution)/shard_map/pallas_call | solution.py:197
Async XLA Ops:
  6.5 49.4 %reduce-scatter.7.cloned.1.call-start = ((), (), s32[]{:S(2)}) async-start(), calls=%async_computation.4 | async-start | bytes 1216512
  17.6 94.3 %reduce-scatter.9.cloned.1.call-start = ((), (), s32[]{:S(2)}) async-start(), calls=%async_computation.5 | async-start | bytes 3379200
  32.4 104.6 %all-gather.3.cloned.1.call-start = ((), (), s32[]{:S(2)}) async-start(), calls=%async_computation.2 | async-start | bytes 1216512 | tf_op jit(solution)/shard_map/all_gather | solution.py:229
  62.7 131.8 %all-gather.5.cloned.1.call-start = ((), (), s32[]{:S(2)}) async-start(), calls=%async_computation.3 | async-start | bytes 3379200 | tf_op jit(solution)/shard_map/all_gather | solution.py:231
Sparse Core Ops, SparseCore 0:
  17.8 38.1 reduce-scatter.6
  58.2 53.6 reduce-scatter.8
  113.8 23.1 all-gather.2
  138.4 56.0 all-gather.4
